TPU v7x, 256 devices: a whole 4x4x8 slice. The times are simulated.
256 devices in a mesh: region: 32 (over z, x), shard: 8 (over y, core).
Axes of the slice: x: 4, y: 4, z: 8, core: 2. Of those that a mesh axis runs over, the one named last changes fastest.
Arguments:
- grid_rows: bfloat16 [262144, 1024], P(('region', 'shard')), may hold values from -6 to 6
- node_inputs: bfloat16 [65536, 1024], P(('region', 'shard')), may hold values from -6 to 6
- row_weight: bfloat16 [1024, 512], replicated, may hold values from -0.1875 to 0.1875
- node_weight: bfloat16 [1024, 512], replicated, may hold values from -0.1875 to 0.1875
- edge_bias: float32 [512], replicated, may hold values from -3 to 3
- edge_out_weight: bfloat16 [512, 1024], replicated, may hold values from -0.125 to 0.125
- norm_gain: float32 [1024], replicated, may hold values from 0.5 to 1.5
- attn_weight: bfloat16 [1024, 3072], replicated
- attn_out_weight: bfloat16 [1024, 1024], replicated, may hold values from -0.1875 to 0.1875
- edge_source: int32 [4096, 128], P(('region', 'shard')), may hold values from 0 to 1023
- edge_target: int32 [4096, 128], P(('region', 'shard')), may hold values from 0 to 255
- block_count: int32 [256], P(('region', 'shard')), may hold values from 1 to 16, as said below
Outputs:
- mixed: bfloat16 [65536, 1024], P(('region', 'shard'))
Inputs may be any that keep to these rules, and one draw needn't show every extreme that they name: `block_count`: some tile uses all 16 blocks. `edge_source`: blocks at or after a tile's block_count are never read.
All inputs are finite; a program needn't handle non-finite values.
Results may differ from a plain program's by a relative error of at most 0.0061.
Values may be sent and summed in bfloat16 or wider, within the bound.
A program may use at most 64 MiB of HBM per device.

v0:
```python
import functools

import jax
import jax.numpy as jnp
from jax import lax
from jax.experimental import pallas as pl
from jax.experimental.pallas import tpu as pltpu
from jax.sharding import PartitionSpec as P

HALF = 560
KEYS = 1408
OWN = 560
PLACES = {-1: (304, 256), 1: (816, 256), -2: (48, 256), 2: (1072, 256), -3: (0, 48), 3: (1328, 80)}
SLOTS = tuple(PLACES)
GRID_COPIES = 4
ACROSS = 4
LOG2E = 1.4426950408889634
F32 = jnp.float32
BF16 = jnp.bfloat16
MESH = pl.DeviceIdType.MESH


def dot(a, b):
    return jnp.dot(a, b, preferred_element_type=F32)


def span_of(start, size, unit):
    return pl.ds(pl.multiple_of(start, unit), size)


def encode_kernel(
    regions,
    shards,
    used,
    source,
    target,
    bias,
    gain,
    grid_hbm,
    nodes_hbm,
    row_hbm,
    node_hbm,
    edge_hbm,
    attn_hbm,
    queries,
    keys,
    values,
    state,
    bounds,
    grid,
    row_weight,
    node_weight,
    edge_weight,
    attn_weight,
    projected,
    table,
    onehot,
    picks,
    hidden,
    sums,
    nodes,
    load_sem,
    row_send,
    row_recv,
    node_send,
    node_recv,
    sum_send,
    sum_recv,
):
    rows, width = grid.shape
    tile = state.shape[0]
    blocks, edges = source.shape
    part = rows // regions
    tiles = regions * shards
    region, shard = lax.axis_index("region"), lax.axis_index("shard")
    me = region * shards + shard

    def there(away):
        return (me + away >= 0) & (me + away < tiles)

    def device(away):
        return ((me + away) // shards, lax.rem(me + away, shards))

    def peer(step):
        return lax.rem(region + step, regions)

    loads = []
    piece = rows // GRID_COPIES

    def load(source_ref, target_ref):
        copy = pltpu.make_async_copy(source_ref, target_ref, load_sem.at[len(loads)])
        copy.start()
        loads.append(copy)
        return copy

    row_load = load(row_hbm, row_weight)
    grid_loads = [
        load(grid_hbm.at[pl.ds(i * piece, piece), :], grid.at[pl.ds(i * piece, piece), :])
        for i in range(GRID_COPIES)
    ]
    node_load = load(nodes_hbm, nodes.at[pl.ds(OWN, tile), :])
    node_weight_load = load(node_hbm, node_weight)
    edge_load = load(edge_hbm, edge_weight)
    attn_load = load(attn_hbm, attn_weight)

    barrier = pltpu.get_barrier_semaphore()
    for step in range(1, regions):
        pl.semaphore_signal(barrier, inc=1, device_id=(peer(step), shard), device_id_type=MESH)
    for away in SLOTS:
        near = lax.rem(me + away + tiles, tiles)
        pl.semaphore_signal(
            barrier, inc=1, device_id=(near // shards, lax.rem(near, shards)), device_id_type=MESH
        )

    row_load.wait()
    for i in range(GRID_COPIES):
        grid_loads[i].wait()
        projected[pl.ds(i * piece, piece), :] = dot(
            grid[pl.ds(i * piece, piece), :], row_weight[...]
        ).astype(BF16)
    node_load.wait()

    pl.semaphore_wait(barrier, regions - 1 + len(SLOTS))

    here = span_of(region * part, part, part)
    row_copies = []
    for step in sorted(range(1, regions), key=lambda k: -min(k, regions - k)):
        copy = pltpu.make_async_remote_copy(
            projected.at[span_of(peer(step) * part, part, part), :],
            table.at[here, :],
            row_send.at[step - 1],
            row_recv.at[step - 1],
            device_id=(peer(step), shard),
            device_id_type=MESH,
        )
        copy.start()
        row_copies.append(copy)

    first_core = lax.rem(shard, 2) == 0
    partner = 1 - 2 * lax.rem(shard, 2)

    def halo(kind, slot, away, first):
        held, sends, receives = kind
        row, count = PLACES[slot]
        at = SLOTS.index(slot)
        return pltpu.make_async_remote_copy(
            held.at[pl.ds(first, count), :],
            held.at[pl.ds(row, count), :],
            sends.at[at],
            receives.at[at],
            device_id=device(away),
            device_id_type=MESH,
        )

    node_halo = (nodes, node_send, node_recv)
    sum_halo = (sums, sum_send, sum_recv)

    def first_copies(kind):
        return [
            (there(2), halo(kind, -2, 2, OWN)),
            (there(-2), halo(kind, 2, -2, OWN)),
            (first_core, halo(kind, -1, 1, OWN)),
            (jnp.logical_not(first_core), halo(kind, 1, -1, OWN)),
        ]

    def forwards(kind, came):
        if came < 0:
            return [
                (there(-2) & jnp.logical_not(first_core), halo(kind, -1, -1, PLACES[-2][0])),
                (there(-2) & there(1), halo(kind, -3, 1, PLACES[-2][0] + tile - PLACES[-3][1])),
            ]
        return [
            (there(2) & first_core, halo(kind, 1, 1, PLACES[2][0])),
            (there(2) & there(-1), halo(kind, 3, -1, PLACES[2][0])),
        ]

    def start(copies):
        for condition, copy in copies:
            pl.when(condition)(copy.start)

    start(first_copies(node_halo))

    table[here, :] = projected[here, :]
    node_weight_load.wait()
    table[pl.ds(rows, tile), :] = (
        dot(nodes[pl.ds(OWN, tile), :], node_weight[...]) + bias[...]
    ).astype(BF16)
    source_cols = jnp.transpose(source[...])
    target_cols = jnp.transpose(target[...])
    lane_rows = lax.broadcasted_iota(jnp.int32, (edges, rows), 1)
    lane_tile = lax.broadcasted_iota(jnp.int32, (edges, tile), 1)
    sub_tile = lax.broadcasted_iota(jnp.int32, (tile, edges), 0)
    limit = jnp.full((1, edges), used[0], jnp.int32)
    for block in range(blocks):
        span = pl.ds(block * edges, edges)
        onehot[span, pl.ds(0, rows)] = (
            (source_cols[:, block : block + 1] == lane_rows).astype(F32).astype(BF16)
        )
        onehot[span, pl.ds(rows, tile)] = (
            (target_cols[:, block : block + 1] == lane_tile).astype(F32).astype(BF16)
        )
        goal = jnp.where(limit > block, target[block : block + 1, :], -1)
        picks[:, span] = (goal == sub_tile).astype(F32).astype(BF16)

    for copy in row_copies:
        copy.wait()
    step_edges = 2 * edges
    for index in range(blocks * edges // step_edges):
        span = pl.ds(index * step_edges, step_edges)
        pre = dot(onehot[span, :], table[...])
        hidden[span, :] = (0.5 * pre * (1.0 + jnp.tanh(0.5 * pre))).astype(BF16)
    sums[pl.ds(OWN, tile), :] = dot(picks[...], hidden[...]).astype(BF16)
    start(first_copies(sum_halo))

    edge_load.wait()
    attn_load.wait()

    def take(ref, spans):
        return jnp.concatenate([ref[span, :] for span in spans], axis=0)

    def normalised(spans):
        held = take(nodes, spans).astype(F32) + dot(take(sums, spans), edge_weight[...])
        held = held.astype(BF16)
        wide = held.astype(F32)
        centred = wide - jnp.mean(wide, axis=1, keepdims=True)
        spread = jnp.mean(centred * centred, axis=1, keepdims=True)
        return held, (centred * lax.rsqrt(spread + 1e-05) * gain[...]).astype(BF16)

    def project(normed, spans, flags):
        key = dot(normed, attn_weight[:, width : 2 * width])
        value = dot(normed, attn_weight[:, 2 * width :])
        begin = 0
        for span, flag in zip(spans, flags):
            rows_in = slice(begin, begin + span.size)
            begin += span.size
            for pair in range(width // 128):
                lanes = slice(pair * 128, pair * 128 + 128)
                keys[pair, span, :] = key[rows_in, lanes].astype(BF16)
                some = value[rows_in, lanes]
                values[pair, span, :] = (some if flag is None else some * flag).astype(BF16)
        return (
            jnp.max(key * key, axis=0, keepdims=True),
            jnp.max(jnp.abs(value), axis=0, keepdims=True),
        )

    own = pl.ds(OWN, tile)
    held, normed = normalised([own])
    state[...] = held
    query = dot(normed, attn_weight[:, :width]) * (LOG2E * 0.125)
    for pair in range(width // 128):
        queries[pair, :, :] = query[:, pair * 128 : pair * 128 + 128].astype(BF16)
    tops = project(normed, [own], [None])
    heads = (
        lax.broadcasted_iota(jnp.int32, (width, 128), 0) // 64
        == lax.broadcasted_iota(jnp.int32, (width, 128), 1)
    )
    heads = heads.astype(F32).astype(BF16)
    query_norm = jnp.max(dot((query * query).astype(BF16), heads), axis=0, keepdims=True)

    def arrive(slot):
        row, count = PLACES[slot]
        span = pl.ds(row, count)

        @pl.when(there(slot))
        def _():
            halo(node_halo, slot, 0, row).wait_recv()
            halo(sum_halo, slot, 0, row).wait_recv()

        @pl.when(jnp.logical_not(there(slot)))
        def _():
            nodes[span, :] = nodes[pl.ds(OWN, count), :]
            sums[span, :] = sums[pl.ds(OWN, count), :]

    def encode(spans, flags, tops):
        _, normed = normalised(spans)
        return tuple(jnp.maximum(a, b) for a, b in zip(tops, project(normed, spans, flags)))

    def choose(picks):
        row, flag = jnp.int32(0), F32(0)
        for condition, slot in picks:
            if abs(slot) == 1:
                pl.when(condition)(functools.partial(arrive, slot))
            row = jnp.where(condition, PLACES[slot][0], row)
            flag = jnp.where(condition, there(slot).astype(F32), flag)
        return [pl.ds(pl.multiple_of(row, 16), tile)], [flag]

    def far(slot):
        arrive(slot)
        for condition, copy in forwards(node_halo, slot) + forwards(sum_halo, slot):
            pl.when(condition)(copy.start)

    second_core = jnp.logical_not(first_core)
    tops = encode(*choose([(first_core, 1), (second_core, -1)]), tops)
    across, down = lax.rem(region, ACROSS), shard // 2
    late_low = (across == 0) & (down == 0)
    late_high = jnp.logical_not(late_low)
    crossing = late_low | ((across == ACROSS - 1) & (down == shards // 2 - 1))

    def far_late(condition):
        pl.when(condition & late_low)(functools.partial(far, -2))
        pl.when(condition & late_high)(functools.partial(far, 2))

    pl.when(late_low)(functools.partial(far, 2))
    pl.when(late_high)(functools.partial(far, -2))
    far_late(jnp.logical_not(crossing))
    row = jnp.where(late_low, PLACES[2][0], PLACES[-2][0])
    flag = jnp.where(late_low, there(2).astype(F32), there(-2).astype(F32))
    tops = encode([pl.ds(pl.multiple_of(row, 16), tile)], [flag], tops)
    early = late_low ^ first_core
    far_late(crossing & jnp.logical_not(early))
    tops = encode(
        *choose(
            [
                (early & first_core, -1),
                (early & second_core, 1),
                (jnp.logical_not(early) & late_low, -2),
                (jnp.logical_not(early) & late_high, 2),
            ]
        ),
        tops,
    )
    far_late(crossing & early)
    tops = encode(
        *choose(
            [
                (jnp.logical_not(early) & first_core, -1),
                (jnp.logical_not(early) & second_core, 1),
                (early & late_low, -2),
                (early & late_high, 2),
            ]
        ),
        tops,
    )
    last = [-3, 3]
    for slot in last:
        arrive(slot)
    tops = encode([pl.ds(*PLACES[slot]) for slot in last], [there(slot).astype(F32) for slot in last], tops)

    top_key, top_value = tops
    key_norm = dot(jnp.broadcast_to(top_key, (8, width)).astype(BF16), heads)
    bounds[0:8, :] = query_norm * key_norm
    bounds[8:16, :] = jnp.broadcast_to(jnp.max(top_value, axis=1, keepdims=True), (8, 128))
    for kind in (node_halo, sum_halo):
        for condition, copy in first_copies(kind) + forwards(kind, -2) + forwards(kind, 2):
            pl.when(condition)(copy.wait_send)


def window_kernel(
    bounds, queries, keys, values, state, out_hbm, mixed,
    out_weight, attended, ones, sem,
):
    pairs, tile, lanes = queries.shape
    half = tile // 2
    span_keys = KEYS - half
    tiles = lax.axis_size("region") * lax.axis_size("shard")
    me = lax.axis_index("region") * lax.axis_size("shard") + lax.axis_index("shard")

    weight_copy = pltpu.make_async_copy(out_hbm, out_weight, sem)
    weight_copy.start()

    spot = lax.broadcasted_iota(jnp.int32, (KEYS, lanes), 0) - OWN + me * tile
    ones[...] = ((spot >= 0) & (spot < tiles * tile)).astype(F32).astype(BF16)
    lane = lax.broadcasted_iota(jnp.int32, (half, lanes), 1)
    row = lax.broadcasted_iota(jnp.int32, (2 * half, lanes), 0) % half
    key = lax.broadcasted_iota(jnp.int32, (2 * half, lanes), 1)
    low = key >= row
    edge = (2 * HALF) // lanes * lanes
    high = [key + at < row + 2 * HALF for at in range(edge, span_keys, lanes)]
    small = jnp.max(bounds[0:8, :]) < 6400.0
    small = small & (jnp.max(bounds[8:16, :]) < 1e9)

    def attend(pair, part, with_max):
        rows = slice(part * half, part * half + half)
        query = queries[pair, rows, :]
        zero = jnp.zeros_like(query)
        query = jnp.concatenate(
            [jnp.where(lane < 64, query, zero), jnp.where(lane >= 64, query, zero)], axis=0
        )
        near = pl.ds(part * half, span_keys)
        scores = lax.dot_general(
            query, keys[pair, near, :], (((1,), (1,)), ((), ())), preferred_element_type=F32
        )
        scores = jnp.concatenate(
            [jnp.where(low, scores[:, :lanes], -1e30), scores[:, lanes:edge]]
            + [
                jnp.where(keep, scores[:, edge + i * lanes : edge + (i + 1) * lanes], -1e30)
                for i, keep in enumerate(high)
            ],
            axis=1,
        )
        if with_max:
            scores = scores - jnp.max(scores, axis=1, keepdims=True)
            raised = jnp.exp2(scores)
            live = lax.dot_general(
                raised.astype(BF16), ones[near, :], (((1,), (0,)), ((), ())),
                preferred_element_type=F32,
            )
            weights = (raised / live[:, 0:1]).astype(BF16)
            both = dot(weights, values[pair, near, :])
        else:
            raised = jnp.exp2(scores).astype(BF16)
            both = dot(raised, jnp.concatenate([values[pair, near, :], ones[near, :]], axis=1))
            both = both[:, :lanes] / both[:, lanes:]
        attended[rows, span_of(pair * lanes, lanes, lanes)] = jnp.where(
            lane < 64, both[:half], both[half:]
        ).astype(BF16)

    def both_halves(with_max, pair, carry):
        for part in range(2):
            attend(pair, part, with_max)
        return carry

    @pl.when(small)
    def _():
        lax.fori_loop(0, pairs, functools.partial(both_halves, False), 0, unroll=4)

    @pl.when(jnp.logical_not(small))
    def _():
        lax.fori_loop(0, pairs, functools.partial(both_halves, True), 0)

    weight_copy.wait()
    mixed[...] = (state[...].astype(F32) + dot(attended[...], out_weight[...])).astype(BF16)


VMEM = pl.BlockSpec(memory_space=pltpu.VMEM)
ANY = pl.BlockSpec(memory_space=pl.ANY)


def local(
    grid_rows,
    node_inputs,
    row_weight,
    node_weight,
    edge_bias,
    edge_out_weight,
    norm_gain,
    attn_weight,
    attn_out_weight,
    edge_source,
    edge_target,
    block_count,
):
    tile, width = node_inputs.shape
    rows = grid_rows.shape[0]
    hidden = row_weight.shape[1]
    blocks, edges = edge_source.shape
    regions, shards = lax.axis_size("region"), lax.axis_size("shard")
    pairs = width // 128
    dma = pltpu.SemaphoreType.DMA
    queries, keys, values, state, bounds = pl.pallas_call(
        functools.partial(encode_kernel, regions, shards),
        out_shape=(
            pltpu.VMEM((pairs, tile, 128), BF16),
            pltpu.VMEM((pairs, KEYS, 128), BF16),
            pltpu.VMEM((pairs, KEYS, 128), BF16),
            pltpu.VMEM((tile, width), BF16),
            jax.ShapeDtypeStruct((16, 128), F32),
        ),
        in_specs=[pl.BlockSpec(memory_space=pltpu.SMEM)] + [VMEM] * 4 + [ANY] * 6,
        out_specs=[VMEM] * 5,
        scratch_shapes=[
            pltpu.VMEM((rows, width), BF16),
            pltpu.VMEM(row_weight.shape, BF16),
            pltpu.VMEM(node_weight.shape, BF16),
            pltpu.VMEM(edge_out_weight.shape, BF16),
            pltpu.VMEM(attn_weight.shape, BF16),
            pltpu.VMEM((rows, hidden), BF16),
            pltpu.VMEM((rows + tile, hidden), BF16),
            pltpu.VMEM((blocks * edges, rows + tile), BF16),
            pltpu.VMEM((tile, blocks * edges), BF16),
            pltpu.VMEM((blocks * edges, hidden), BF16),
            pltpu.VMEM((KEYS, hidden), BF16),
            pltpu.VMEM((KEYS, width), BF16),
            dma((GRID_COPIES + 5,)),
            dma((regions - 1,)),
            dma((regions - 1,)),
            dma((len(SLOTS),)),
            dma((len(SLOTS),)),
            dma((len(SLOTS),)),
            dma((len(SLOTS),)),
        ],
        compiler_params=pltpu.CompilerParams(
            collective_id=0, has_side_effects=True, vmem_limit_bytes=57 * 2**20
        ),
        name="encode",
    )(
        block_count,
        edge_source,
        edge_target,
        edge_bias[None],
        norm_gain[None],
        grid_rows,
        node_inputs,
        row_weight,
        node_weight,
        edge_out_weight,
        attn_weight,
    )
    return pl.pallas_call(
        window_kernel,
        out_shape=jax.ShapeDtypeStruct((tile, width), BF16),
        in_specs=[VMEM] * 5 + [ANY],
        out_specs=VMEM,
        scratch_shapes=[
            pltpu.VMEM((width, width), BF16),
            pltpu.VMEM((tile, width), BF16),
            pltpu.VMEM((KEYS, 128), BF16),
            dma,
        ],
        compiler_params=pltpu.CompilerParams(vmem_limit_bytes=57 * 2**20),
        name="window",
    )(bounds, queries, keys, values, state, attn_out_weight)


def solution(mesh):
    placed = (
        P(("region", "shard"), None),
        P(("region", "shard"), None),
        P(),
        P(),
        P(),
        P(),
        P(),
        P(),
        P(),
        P(("region", "shard"), None),
        P(("region", "shard"), None),
        P(("region", "shard")),
    )
    return jax.shard_map(
        local, mesh=mesh, in_specs=placed, out_specs=P(("region", "shard"), None), check_vma=False
    )
```

profile of v0, /device:TPU:32, one launch (start us, length us, event | category | flops | bytes accessed | tf_op | source)
XLA Modules:
  0.0 87.7 jit_solution(11129988578838882567)
XLA Ops:
  0.7 61.2 %encode.1 = (bf16[8,256,128]{2,1,0:T(8,128)(2,1)S(1)}, bf16[8,1408,128]{2,1,0:T(8,128)(2,1)S(1)}, bf16[8,1408,128]{2,1,0:T(8,128)(2,1)S(1)}, bf16[256,1024]{1,0:T(8,128)(2,1)S(1)}, f32[16,128]{1,0:T(8,128)}) custom-call(s32[1]{0:T(128)S(6)} %copy.13.used, s32[16,128]{1,0:T(8,128)} %source.1, s32[16,128]{1,0:T(8,128)} %target.1, f32[1,512]{1,0:T(1,128)} %bitcast.3, ...), custom_call_target="tpu_custom_call" | custom-call | tf_op jit(solution)/shard_map/encode/pallas_call | solution.py:450
  61.9 0.0 copy-start
  61.9 1.6 %copy-done = bf16[8,1408,128]{2,1,0:T(8,128)(2,1)} copy-done((bf16[8,1408,128]{2,1,0:T(8,128)(2,1)}, bf16[8,1408,128]{2,1,0:T(8,128)(2,1)S(1)}, u32[]{:S(2)}) %copy-start) | copy-done | bytes 2883608
  63.5 0.0 copy-start.1
  63.5 1.6 %copy-done.1 = bf16[8,1408,128]{2,1,0:T(8,128)(2,1)} copy-done((bf16[8,1408,128]{2,1,0:T(8,128)(2,1)}, bf16[8,1408,128]{2,1,0:T(8,128)(2,1)S(1)}, u32[]{:S(2)}) %copy-start.1) | copy-done | bytes 2883608
  65.1 0.0 copy-start.2
  65.1 0.8 copy-done.2
  65.9 0.0 copy-start.3
  65.9 0.8 copy-done.3
  66.7 20.9 %window.1 = bf16[256,1024]{1,0:T(8,128)(2,1)} custom-call(f32[16,128]{1,0:T(8,128)} %get-tuple-element.10.bounds, bf16[8,256,128]{2,1,0:T(8,128)(2,1)} %copy-done.2, bf16[8,1408,128]{2,1,0:T(8,128)(2,1)} %copy-done, bf16[8,1408,128]{2,1,0:T(8,128)(2,1)} %copy-done.1, bf16[256,1024]{1,0:T(8,128)(2,1)} %copy-done.3, bf16[1024,1024]{1,0:T(8,128)(2,1)} %out_hbm.1), custom_call_target="tpu_custom_call" | custom-call | tf_op jit(solution)/shard_map/window/pallas_call | solution.py:499
Async XLA Ops:
  61.9 1.6 %copy-start = (bf16[8,1408,128]{2,1,0:T(8,128)(2,1)}, bf16[8,1408,128]{2,1,0:T(8,128)(2,1)S(1)}, u32[]{:S(2)}) copy-start(bf16[8,1408,128]{2,1,0:T(8,128)(2,1)S(1)} %get-tuple-element.12.keys) | copy-start | bytes 8650756
  63.5 1.6 %copy-start.1 = (bf16[8,1408,128]{2,1,0:T(8,128)(2,1)}, bf16[8,1408,128]{2,1,0:T(8,128)(2,1)S(1)}, u32[]{:S(2)}) copy-start(bf16[8,1408,128]{2,1,0:T(8,128)(2,1)S(1)} %get-tuple-element.13.values) | copy-start | bytes 8650756
  65.1 0.8 copy-start.2
  65.9 0.8 copy-start.3
where the time goes:
time: 87.9 us; the launch traced here: 87.7 us
  Pallas kernels  82.1 us (93%)
  local copies, waits for them, and re-layouts  4.8 us (5%)
    pallas_call x1, Pallas kernels, local(): pl.pallas_call(functools.partial(encode_kernel, regions, shards), out_sha...  61.2 us
    pallas_call x1, Pallas kernels, local(): pl.pallas_call(window_kernel, out_shape=jax.ShapeDtypeStruct((tile, width...  20.9 us
    unnamed x8, local copies, waits for them, and re-layouts  4.8 us

commit v1 on v0

--- a/solution.py
+++ b/solution.py
@@ -42,11 +42,13 @@
     node_hbm,
     edge_hbm,
     attn_hbm,
+    out_hbm,
     queries,
     keys,
     values,
     state,
     bounds,
+    out_weight,
     grid,
     row_weight,
     node_weight,
@@ -102,6 +104,7 @@
     node_weight_load = load(node_hbm, node_weight)
     edge_load = load(edge_hbm, edge_weight)
     attn_load = load(attn_hbm, attn_weight)
+    out_load = load(out_hbm, out_weight)
 
     barrier = pltpu.get_barrier_semaphore()
     for step in range(1, regions):
@@ -214,6 +217,7 @@
 
     edge_load.wait()
     attn_load.wait()
+    out_load.wait()
 
     def take(ref, spans):
         return jnp.concatenate([ref[span, :] for span in spans], axis=0)
@@ -346,17 +350,14 @@
 
 
 def window_kernel(
-    bounds, queries, keys, values, state, out_hbm, mixed,
-    out_weight, attended, ones, sem,
+    bounds, queries, keys, values, state, out_weight, mixed,
+    attended, ones,
 ):
     pairs, tile, lanes = queries.shape
     half = tile // 2
     span_keys = KEYS - half
     tiles = lax.axis_size("region") * lax.axis_size("shard")
     me = lax.axis_index("region") * lax.axis_size("shard") + lax.axis_index("shard")
-
-    weight_copy = pltpu.make_async_copy(out_hbm, out_weight, sem)
-    weight_copy.start()
 
     spot = lax.broadcasted_iota(jnp.int32, (KEYS, lanes), 0) - OWN + me * tile
     ones[...] = ((spot >= 0) & (spot < tiles * tile)).astype(F32).astype(BF16)
@@ -418,7 +419,6 @@
     def _():
         lax.fori_loop(0, pairs, functools.partial(both_halves, True), 0)
 
-    weight_copy.wait()
     mixed[...] = (state[...].astype(F32) + dot(attended[...], out_weight[...])).astype(BF16)
 
 
@@ -447,17 +447,18 @@
     regions, shards = lax.axis_size("region"), lax.axis_size("shard")
     pairs = width // 128
     dma = pltpu.SemaphoreType.DMA
-    queries, keys, values, state, bounds = pl.pallas_call(
+    queries, keys, values, state, bounds, out_weight = pl.pallas_call(
         functools.partial(encode_kernel, regions, shards),
         out_shape=(
             pltpu.VMEM((pairs, tile, 128), BF16),
             pltpu.VMEM((pairs, KEYS, 128), BF16),
             pltpu.VMEM((pairs, KEYS, 128), BF16),
             pltpu.VMEM((tile, width), BF16),
-            jax.ShapeDtypeStruct((16, 128), F32),
+            pltpu.VMEM((16, 128), F32),
+            pltpu.VMEM((width, width), BF16),
         ),
-        in_specs=[pl.BlockSpec(memory_space=pltpu.SMEM)] + [VMEM] * 4 + [ANY] * 6,
-        out_specs=[VMEM] * 5,
+        in_specs=[pl.BlockSpec(memory_space=pltpu.SMEM)] + [VMEM] * 4 + [ANY] * 7,
+        out_specs=[VMEM] * 6,
         scratch_shapes=[
             pltpu.VMEM((rows, width), BF16),
             pltpu.VMEM(row_weight.shape, BF16),
@@ -471,7 +472,7 @@
             pltpu.VMEM((blocks * edges, hidden), BF16),
             pltpu.VMEM((KEYS, hidden), BF16),
             pltpu.VMEM((KEYS, width), BF16),
-            dma((GRID_COPIES + 5,)),
+            dma((GRID_COPIES + 6,)),
             dma((regions - 1,)),
             dma((regions - 1,)),
             dma((len(SLOTS),)),
@@ -480,7 +481,7 @@
             dma((len(SLOTS),)),
         ],
         compiler_params=pltpu.CompilerParams(
-            collective_id=0, has_side_effects=True, vmem_limit_bytes=57 * 2**20
+            collective_id=0, has_side_effects=True, vmem_limit_bytes=55 * 2**20
         ),
         name="encode",
     )(
@@ -495,21 +496,20 @@
         node_weight,
         edge_out_weight,
         attn_weight,
+        attn_out_weight,
     )
     return pl.pallas_call(
         window_kernel,
         out_shape=jax.ShapeDtypeStruct((tile, width), BF16),
-        in_specs=[VMEM] * 5 + [ANY],
+        in_specs=[VMEM] * 6,
         out_specs=VMEM,
         scratch_shapes=[
-            pltpu.VMEM((width, width), BF16),
             pltpu.VMEM((tile, width), BF16),
             pltpu.VMEM((KEYS, 128), BF16),
-            dma,
         ],
-        compiler_params=pltpu.CompilerParams(vmem_limit_bytes=57 * 2**20),
+        compiler_params=pltpu.CompilerParams(vmem_limit_bytes=24 * 2**20),
         name="window",
-    )(bounds, queries, keys, values, state, attn_out_weight)
+    )(bounds, queries, keys, values, state, out_weight)
 
 
 def solution(mesh):

time: 87.9 us -> 79.3 us (0.902)
  local copies, waits for them, and re-layouts: 4.8 us -> 0 us
  Pallas kernels: 82.1 us -> 78.5 us
    unnamed x8 -> x0, local copies, waits for them, and re-layouts: 4.8 us -> none
    pallas_call x1, Pallas kernels: 20.9 us -> 17.8 us  [local(): pl.pallas_call(window_kernel, out_shape=jax.ShapeDtypeStruct((tile, width...]
where the time goes in v1:
time: 79.3 us; the launch traced here: 79.1 us
  Pallas kernels  78.5 us (99%)
    pallas_call x1, Pallas kernels, local(): pl.pallas_call(functools.partial(encode_kernel, regions, shards), out_sha...  60.6 us
    pallas_call x1, Pallas kernels, local(): pl.pallas_call(window_kernel, out_shape=jax.ShapeDtypeStruct((tile, width...  17.8 us

profile of v1, /device:TPU:32, one launch (start us, length us, event | category | flops | bytes accessed | tf_op | source)
XLA Modules:
  0.0 79.1 jit_solution(12119366707906556389)
XLA Ops:
  0.7 60.6 %encode.1 = (bf16[8,256,128]{2,1,0:T(8,128)(2,1)S(1)}, bf16[8,1408,128]{2,1,0:T(8,128)(2,1)S(1)}, bf16[8,1408,128]{2,1,0:T(8,128)(2,1)S(1)}, bf16[256,1024]{1,0:...) custom-call(s32[1]{0:T(128)S(6)} %copy.13.used, s32[16,128]{1,0:T(8,128)} %source.1, ...), custom_call_target="tpu_custom_call" | custom-call | tf_op jit(solution)/shard_map/encode/pallas_call | solution.py:450
  61.3 17.8 %window.1 = bf16[256,1024]{1,0:T(8,128)(2,1)} custom-call(f32[16,128]{1,0:T(8,128)S(1)} %get-tuple-element.11.bounds, bf16[8,256,128]{2,1,0:T(8,128)(2,1)S(1)} %get-tuple-element.12.queries, bf16[8,1408,128]{2,1,0:T(8,128)(2,1)S(1)} %get-tuple-element.13.keys, bf16[8,1408,128]{2,1,0:T(8,128)(2,1)S(1)} %get-tuple-element.14.values, ...), custom_call_target="tpu_custom_call" | custom-call | tf_op jit(solution)/shard_map/window/pallas_call | solution.py:501

commit v2 on v1

--- a/solution.py
+++ b/solution.py
@@ -413,7 +413,7 @@
 
     @pl.when(small)
     def _():
-        lax.fori_loop(0, pairs, functools.partial(both_halves, False), 0, unroll=4)
+        lax.fori_loop(0, pairs, functools.partial(both_halves, False), 0, unroll=8)
 
     @pl.when(jnp.logical_not(small))
     def _():

time: 79.3 us -> 79.6 us (level)
  no operation moved by 1% of the time
where the time goes in v2:
time: 79.6 us; the launch traced here: 79.4 us
  Pallas kernels  78.7 us (99%)
    pallas_call x1, Pallas kernels, local(): pl.pallas_call(functools.partial(encode_kernel, regions, shards), out_sha...  60.6 us
    pallas_call x1, Pallas kernels, local(): pl.pallas_call(window_kernel, out_shape=jax.ShapeDtypeStruct((tile, width...  18.1 us

profile of v2, /device:TPU:32, one launch (start us, length us, event | category | flops | bytes accessed | tf_op | source)
XLA Modules:
  0.0 79.4 jit_solution(5257976198353371313)
XLA Ops:
  0.7 60.6 %encode.1 = (bf16[8,256,128]{2,1,0:T(8,128)(2,1)S(1)}, bf16[8,1408,128]{2,1,0:T(8,128)(2,1)S(1)}, bf16[8,1408,128]{2,1,0:T(8,128)(2,1)S(1)}, bf16[256,1024]{1,0:...) custom-call(s32[1]{0:T(128)S(6)} %copy.13.used, s32[16,128]{1,0:T(8,128)} %source.1, ...), custom_call_target="tpu_custom_call" | custom-call | tf_op jit(solution)/shard_map/encode/pallas_call | solution.py:450
  61.3 18.1 %window.1 = bf16[256,1024]{1,0:T(8,128)(2,1)} custom-call(f32[16,128]{1,0:T(8,128)S(1)} %get-tuple-element.11.bounds, bf16[8,256,128]{2,1,0:T(8,128)(2,1)S(1)} %get-tuple-element.12.queries, bf16[8,1408,128]{2,1,0:T(8,128)(2,1)S(1)} %get-tuple-element.13.keys, bf16[8,1408,128]{2,1,0:T(8,128)(2,1)S(1)} %get-tuple-element.14.values, ...), custom_call_target="tpu_custom_call" | custom-call | tf_op jit(solution)/shard_map/window/pallas_call | solution.py:501
